TPU v7x, 512 devices: a whole 4x4x16 slice. The times are simulated.
512 devices in a mesh: row: 16 (over y, x), col: 32 (over z, core).
Axes of the slice: x: 4, y: 4, z: 16, core: 2. Of those that a mesh axis runs over, the one named last changes fastest.
Arguments:
- momentum: float32 [4096, 14336], P('row', 'col'), may hold values from -6 to 6
- grads: bfloat16 [1, 4096, 14336], P(None, 'row', 'col'), may hold values from -6 to 6
- right_factor: float32 [128, 14336], P(None, 'col'), may hold values from -0.046875 to 0.046875
Outputs:
- new_momentum: float32 [4096, 14336], P('row', 'col')
- new_factor: float32 [128, 14336], P(None, 'col')
- update: float32 [4096, 14336], P('row', 'col')
All inputs are finite; a program needn't handle non-finite values.
Results may differ from a plain program's by a relative error of at most 0.0005.
Values sent between devices are 32-bit elements; how exact they have to be, the bound alone decides.
A program may use at most 64 MiB of HBM per device.

v0:
```python
import jax
import jax.numpy as jnp
from jax import lax
from jax.sharding import PartitionSpec as P

M = 4096
N = 14336
RANK = 128
POWER = 2


DECAY_LEFT = 0.05
EPSILON = 1e-06


def contract(first, second, first_dim, second_dim):
    return lax.dot_general(
        first,
        second,
        (((first_dim,), (second_dim,)), ((), ())),
        precision=lax.Precision.HIGHEST,
        preferred_element_type=jnp.float32,
    )


def orthonormal(gram_matrix, left_t):
    lower_f = jnp.linalg.cholesky(gram_matrix)
    return lax.linalg.triangular_solve(lower_f, left_t, left_side=True, lower=True)


def local(momentum, grads, right_factor):
    factor_t = right_factor
    moment = momentum
    blend = moment + grads[0].astype(jnp.float32)
    for sweep_index in range(POWER):
        partial_value = contract(factor_t, blend, 1, 1)
        left_t = lax.psum(partial_value, "col")
        gram_matrix = lax.psum(contract(left_t, left_t, 1, 1), "row")
        left_t = orthonormal(gram_matrix, left_t)
        right_t = lax.psum(contract(left_t, blend, 1, 0), "row")
        squares = lax.psum(jnp.sum(right_t * right_t, axis=1, keepdims=True), "col")
        factor_t = right_t / (jnp.sqrt(squares) + EPSILON)
    moment = blend - DECAY_LEFT * contract(left_t, right_t, 0, 0)
    accum = contract(left_t, factor_t, 0, 0)
    return (moment, factor_t, accum * jnp.float32((M * N / RANK) ** 0.5))


def solution(mesh):
    return jax.shard_map(
        local,
        mesh=mesh,
        in_specs=(P("row", "col"), P(None, "row", "col"), P(None, "col")),
        out_specs=(P("row", "col"), P(None, "col"), P("row", "col")),
        check_vma=False,
    )
```

profile of v0, /device:TPU:1, one launch (start us, length us, event | category | flops | bytes accessed | tf_op | source)
XLA Modules:
  0.0 1026.8 jit_solution(11263512012418945397)
XLA Ops:
  7.2 0.0 copy-start
  7.2 0.0 all-reduce.7.cloned.1.call-start
  7.2 0.9 copy-done
  8.1 2.7 convolution_bitcast_fusion
  10.8 0.0 all-reduce.7.cloned.1.call-update
  10.9 0.0 all-reduce.9.cloned.1.call-start
  10.9 204.7 %all-reduce.7.cloned.1.call-done = f32[128,256]{0,1:T(8,128)} async-done(((f32[128,256]{0,1:T(8,128)}), f32[128,256]{0,1:T(8,128)}) %all-reduce.7.cloned.1.call-update) | async-done | bytes 131088 | tf_op jit(solution)/shard_map/psum | solution.py:37
  215.6 2.0 fusion.16
  217.6 0.0 all-reduce.9.cloned.1.call-update
  217.6 0.0 all-reduce.11.cloned.1.call-start
  217.7 108.6 %all-reduce.9.cloned.1.call-done = f32[128,128]{0,1:T(8,128)} async-done(((f32[128,128]{0,1:T(8,128)}), f32[128,128]{0,1:T(8,128)}) %all-reduce.9.cloned.1.call-update) | async-done | bytes 65552 | tf_op jit(solution)/shard_map/psum | solution.py:38
  326.3 0.9 copy.7
  327.2 0.9 fusion.11
  328.1 0.0 copy-start.4
  328.1 11.7 %cholesky.44 = f32[128,128]{1,0:T(8,128)S(1)} custom-call(f32[128,128]{1,0:T(8,128)S(1)} %fusion.11), custom_call_target="Cholesky" | custom-call | tf_op jit(solution)/shard_map/jit(cholesky)/cholesky | solution.py:27
  339.8 0.6 compare_reduce_fusion.1
  340.5 0.7 fusion.4
  341.2 9.8 custom-call.6
  351.0 0.3 fusion.9
  351.3 1.2 fusion.15
  352.6 0.0 all-reduce.11.cloned.1.call-update
  352.6 0.0 all-reduce.13.cloned.1.call-start
  352.6 115.1 %all-reduce.11.cloned.1.call-done = f32[128,448]{0,1:T(8,128)} async-done(((f32[128,448]{0,1:T(8,128)}), f32[128,448]{0,1:T(8,128)}) %all-reduce.11.cloned.1.call-update) | async-done | bytes 229392 | tf_op jit(solution)/shard_map/psum | solution.py:40
  467.7 1.1 multiply_reduce_fusion.1
  468.8 48.9 %psum.59 = f32[128,1]{0,1:T(1,128)S(1)} all-reduce(f32[128,1]{0,1:T(1,128)S(1)} %bitcast.48), channel_id=1, replica_groups=mesh['row'=16,'col'=32] {'col'}, use_global_device_ids=true, to_apply=%region_6.9 | all-reduce | flops 128 | bytes 1024 | tf_op jit(solution)/shard_map/psum | solution.py:41
  517.7 1.3 fusion.1
  519.0 0.0 all-reduce.13.cloned.1.call-update
  519.0 0.0 all-reduce.15.cloned.1.call-start
  519.1 197.1 %all-reduce.13.cloned.1.call-done = f32[128,256]{1,0:T(8,128)} async-done(((f32[128,256]{1,0:T(8,128)}), f32[128,256]{1,0:T(8,128)}) %all-reduce.13.cloned.1.call-update) | async-done | bytes 131088 | tf_op jit(solution)/shard_map/psum | solution.py:37
  716.2 1.9 fusion.17
  718.0 0.0 all-reduce.15.cloned.1.call-update
  718.1 0.2 all-reduce.17.cloned.1.call-start
  718.3 108.4 %all-reduce.15.cloned.1.call-done = f32[128,128]{0,1:T(8,128)} async-done(((f32[128,128]{0,1:T(8,128)}), f32[128,128]{0,1:T(8,128)}) %all-reduce.15.cloned.1.call-update) | async-done | bytes 65552 | tf_op jit(solution)/shard_map/psum | solution.py:38
  826.7 1.0 copy.9
  827.7 0.0 copy-done.7
  827.8 11.7 %cholesky.55 = f32[128,128]{1,0:T(8,128)S(1)} custom-call(f32[128,128]{1,0:T(8,128)S(1)} %fusion.8), custom_call_target="Cholesky" | custom-call | tf_op jit(solution)/shard_map/jit(cholesky)/cholesky | solution.py:27
  839.5 0.6 compare_reduce_fusion
  840.1 0.7 fusion.5
  840.8 9.8 custom-call.7
  850.6 0.3 fusion.6
  850.9 1.2 fusion.14
  852.2 0.0 all-reduce.17.cloned.1.call-update
  852.2 115.1 %all-reduce.17.cloned.1.call-done = f32[128,448]{0,1:T(8,128)} async-done(((f32[128,448]{0,1:T(8,128)}), f32[128,448]{0,1:T(8,128)}) %all-reduce.17.cloned.1.call-update) | async-done | bytes 229392 | tf_op jit(solution)/shard_map/psum | solution.py:40
  967.3 1.1 multiply_reduce_fusion
  968.4 48.9 %psum.63 = f32[128,1]{0,1:T(1,128)S(1)} all-reduce(f32[128,1]{0,1:T(1,128)S(1)} %bitcast.49), channel_id=1, replica_groups=mesh['row'=16,'col'=32] {'col'}, use_global_device_ids=true, to_apply=%region_11.14 | all-reduce | flops 128 | bytes 1024 | tf_op jit(solution)/shard_map/psum | solution.py:41
  1017.4 0.0 copy-start.6
  1017.4 1.3 convolution_multiply_fusion
  1018.7 1.3 fusion
  (19 shorter events, 0.2 us)
Async XLA Ops:
  7.2 0.9 copy-start
  7.2 208.4 %all-reduce.7.cloned.1.call-start = ((), (), s32[]{:S(2)}) async-start(), calls=%async_computation | async-start | bytes 262144 | tf_op jit(solution)/shard_map/psum | solution.py:37
  10.9 315.4 %all-reduce.9.cloned.1.call-start = ((), (), s32[]{:S(2)}) async-start(), calls=%async_computation.1 | async-start | bytes 131072 | tf_op jit(solution)/shard_map/psum | solution.py:38
  217.6 133.7 %copy-start.1 = (f32[256,448]{0,1:T(8,128)S(1)}, f32[256,448]{0,1:T(8,128)}, u32[]{:S(2)}) copy-start(f32[256,448]{0,1:T(8,128)} %param.6) | copy-start | bytes 1376260
  217.6 250.1 %all-reduce.11.cloned.1.call-start = ((), (), s32[]{:S(2)}) async-start(), calls=%async_computation.2 | async-start | bytes 458752 | tf_op jit(solution)/shard_map/psum | solution.py:40
  328.1 22.9 %copy-start.4 = (f32[128,256]{0,1:T(8,128)S(1)}, f32[128,256]{0,1:T(8,128)}, u32[]{:S(2)}) copy-start(f32[128,256]{0,1:T(8,128)} %all-reduce.7.cloned.1.call-done) | copy-start | bytes 393220
  340.5 10.9 %copy-start.2 = (bf16[1,256,448]{1,2,0:T(8,128)(2,1)S(1)}, bf16[1,256,448]{1,2,0:T(8,128)(2,1)}, u32[]{:S(2)}) copy-start(bf16[1,256,448]{1,2,0:T(8,128)(2,1)} %param.7) | copy-start | bytes 688132
  352.6 363.6 %all-reduce.13.cloned.1.call-start = ((), (), s32[]{:S(2)}) async-start(), calls=%async_computation.3 | async-start | bytes 262144 | tf_op jit(solution)/shard_map/psum | solution.py:37
  467.7 50.0 %copy-start.8 = (f32[128,448]{0,1:T(8,128)S(1)}, f32[128,448]{0,1:T(8,128)}, u32[]{:S(2)}) copy-start(f32[128,448]{0,1:T(8,128)} %all-reduce.11.cloned.1.call-done) | copy-start | bytes 688132
  519.0 307.7 %all-reduce.15.cloned.1.call-start = ((), (), s32[]{:S(2)}) async-start(), calls=%async_computation.4 | async-start | bytes 131072 | tf_op jit(solution)/shard_map/psum | solution.py:38
  718.1 249.3 %all-reduce.17.cloned.1.call-start = ((), (), s32[]{:S(2)}) async-start(), calls=%async_computation.5 | async-start | bytes 458752 | tf_op jit(solution)/shard_map/psum | solution.py:40
  826.7 1.0 copy-start.7
  827.7 22.9 %copy-start.5 = (f32[128,256]{1,0:T(8,128)S(1)}, f32[128,256]{1,0:T(8,128)}, u32[]{:S(2)}) copy-start(f32[128,256]{1,0:T(8,128)} %all-reduce.13.cloned.1.call-done) | copy-start | bytes 393220
  967.3 50.0 %copy-start.3 = (f32[128,448]{0,1:T(8,128)S(1)}, f32[128,448]{0,1:T(8,128)}, u32[]{:S(2)}) copy-start(f32[128,448]{0,1:T(8,128)} %all-reduce.17.cloned.1.call-done) | copy-start | bytes 688132
  1017.4 1.3 copy-start.6
Sparse Core Ops, SparseCore 0:
  11.0 204.5 all-reduce.6
  219.3 106.8 all-reduce.8
  352.7 114.9 all-reduce.10
  519.1 196.9 all-reduce.12
  719.8 106.8 all-reduce.14
  852.3 114.9 all-reduce.16
where the time goes:
time: 1030 us
  waiting for transfers between devices  849 us (82%)
  blocking collectives  97.8 us (9%)
  other arithmetic  48.8 us (5%)
  between operations  14.3 us (1%)
  matrix products  13.5 us (1%)
    psum x2, waiting for transfers between devices, local(): left_t = lax.psum(partial_value, 'col')  402 us
    psum x2, waiting for transfers between devices, local(): right_t = lax.psum(contract(left_t, blend, 1, 0), 'row')  230 us
    psum x2, waiting for transfers between devices, local(): gram_matrix = lax.psum(contract(left_t, left_t, 1, 1), 'row')  217 us
    psum x2, blocking collectives, local(): squares = lax.psum(jnp.sum(right_t * right_t, axis=1, keepdims=True), 'col')  97.8 us
    another operation x6, other arithmetic, orthonormal(): lower_f = jnp.linalg.cholesky(gram_matrix)  24.8 us
    another operation x4, other arithmetic, orthonormal(): lax.linalg.triangular_solve(lower_f, left_t, left_side=True, lower=True)  21 us
  transfers between devices with their start and end apart: 6, of which 6 were waited for; matrix products, arithmetic and copies ran while one was open for 0% of the time, Pallas kernels for 0%

commit v1 on v0

v1 whole, which is shorter than its diff:
```python
import jax
import jax.numpy as jnp
from jax import lax
from jax.experimental import pallas as pl
from jax.experimental.pallas import tpu as pltpu
from jax.sharding import PartitionSpec as P

M = 4096
N = 14336
RANK = 128
POWER = 2

DECAY_LEFT = 0.05
EPSILON = 1e-06
SCALE = (M * N / RANK) ** 0.5

ROWS = 16
COLS = 32
HIGH = 256
WIDE = 448
MESH = pl.DeviceIdType.MESH

TURNS = sorted(
    ((dy, dx) for dy in range(4) for dx in range(4) if dy or dx),
    key=lambda turn: -(min(turn[0], 4 - turn[0]) + min(turn[1], 4 - turn[1])),
)


def contract(first, second, first_dim, second_dim):
    return lax.dot_general(
        first,
        second,
        (((first_dim,), (second_dim,)), ((), ())),
        precision=lax.Precision.HIGHEST,
        preferred_element_type=jnp.float32,
    )


def spread(x):
    return jnp.broadcast_to(x, (8, 128))

def inverse_factor(w):
    lane = lax.broadcasted_iota(jnp.int32, (8, 128), 1)
    sub = lax.broadcasted_iota(jnp.int32, (8, 128), 0)
    for k in range(16):
        base = 8 * k
        tile = w[base:base + 8, :]
        inside = (lane >= base) & (lane < base + 8)
        column = [spread(tile[:, base + t:base + t + 1]) for t in range(8)]
        d = {(i, t): spread(column[t][i:i + 1, :]) for t in range(8) for i in range(t, 8)}
        start = jnp.where(inside, jnp.where(lane - base == sub, 1.0, 0.0), tile)
        rows = [spread(start[i:i + 1, :]) for i in range(8)]
        low, scale = {}, []
        for t in range(8):
            inv = lax.rsqrt(d[t, t])
            scale.append(inv)
            for i in range(t + 1, 8):
                low[i, t] = d[i, t] * inv
            rows[t] = rows[t] * inv
            for i in range(t + 1, 8):
                for j in range(t + 1, i + 1):
                    d[i, j] = d[i, j] - low[i, t] * low[j, t]
                rows[i] = rows[i] - low[i, t] * rows[t]
        block = rows[0]
        for t in range(1, 8):
            block = jnp.where(sub == t, rows[t], block)
        w[base:base + 8, :] = jnp.where(lane < base + 8, block, 0.0)
        if k == 15:
            break
        turned = block.T if k < 14 else None
        for kk in range(k + 1, 16):
            at = 8 * kk
            tile = w[at:at + 8, :]
            if kk == k + 1:
                ls = []
                for t in range(8):
                    x = spread(tile[:, base + t:base + t + 1])
                    for s in range(t):
                        x = x - ls[s] * low[t, s]
                    ls.append(x * scale[t])
            else:
                ls = [spread(turned[at:at + 8, t:t + 1]) for t in range(8)]
            tile = jnp.where(inside, 0.0, tile)
            for t in range(8):
                tile = tile - ls[t] * rows[t]
            w[at:at + 8, :] = tile


def kernel(
    momentum, grads, factor_in, new_momentum, new_factor, update,
    moment_v, grads_v, blend, right, left_part, left_got, left_t,
    gram_part, gram_got, gram, right_part, right_got, right_sum,
    square_own, square_got, factor_v, update_v,
    in_sem, out_sem, left_send, left_recv, gram_send, gram_recv,
    right_send, right_recv, square_send, square_recv,
):
    row = lax.axis_index("row")
    col = lax.axis_index("col")
    y, x = row // 4, row % 4

    col_peers = [(col + 16 + (k + 1) // 2 * (1 if k % 2 else -1) + COLS) % COLS for k in range(31)]
    row_peers = [(y + dy) % 4 * 4 + (x + dx) % 4 for dy, dx in TURNS]

    barrier = pltpu.get_barrier_semaphore()
    for peer in col_peers:
        pl.semaphore_signal(barrier, inc=1, device_id=(row, peer), device_id_type=MESH)
    for peer in row_peers:
        pl.semaphore_signal(barrier, inc=1, device_id=(peer, col), device_id_type=MESH)

    loads = [
        pltpu.make_async_copy(factor_in, right, in_sem.at[0]),
        pltpu.make_async_copy(momentum, moment_v, in_sem.at[1]),
        pltpu.make_async_copy(grads.at[0], grads_v, in_sem.at[2]),
    ]
    for load in loads:
        load.start()
    for load in loads:
        load.wait()
    blend[...] = moment_v[...] + grads_v[...].astype(jnp.float32)

    def remote(src, dst, send, recv, device):
        pltpu.make_async_remote_copy(
            src_ref=src, dst_ref=dst, send_sem=send, recv_sem=recv,
            device_id=device, device_id_type=MESH,
        ).start()

    def await_bytes(ref, sem):
        pltpu.make_async_copy(ref, ref, sem).wait()

    own_col = pl.ds(pl.multiple_of(8 * col, 8), 8)
    own_row = pl.ds(pl.multiple_of(8 * row, 8), 8)

    def sweep(step, carry):
        left_part[step] = contract(blend[...], right[...], 1, 1)

        @pl.when(step == 0)
        def _():
            pl.semaphore_wait(barrier, 46)

        for peer in col_peers:
            part = left_part.at[step, pl.ds(pl.multiple_of(8 * peer, 8), 8)]
            remote(part, left_got.at[step, col], left_send.at[step, 0], left_recv.at[step, 0], (row, peer))
        left_got[step, col] = left_part[step, own_col]
        await_bytes(left_got.at[step, pl.ds(0, COLS - 1)], left_recv.at[step, 0])
        left_t[step, own_col] = jnp.sum(left_got[step], axis=0)
        for peer in col_peers:
            mine = left_t.at[step, own_col]
            remote(mine, mine, left_send.at[step, 1], left_recv.at[step, 1], (row, peer))
        await_bytes(left_t.at[step, pl.ds(0, HIGH - 8)], left_recv.at[step, 1])

        gram_part[step] = contract(left_t[step], left_t[step], 0, 0)
        for peer in row_peers:
            part = gram_part.at[step, pl.ds(pl.multiple_of(8 * peer, 8), 8)]
            remote(part, gram_got.at[step, row], gram_send.at[step, 0], gram_recv.at[step, 0], (peer, col))
        right_part[step] = contract(left_t[step], blend[...], 0, 0)
        for peer in row_peers:
            part = right_part.at[step, pl.ds(pl.multiple_of(8 * peer, 8), 8)]
            remote(part, right_got.at[step, row], right_send.at[step, 0], right_recv.at[step, 0], (peer, col))

        gram_got[step, row] = gram_part[step, own_row]
        await_bytes(gram_got.at[step, pl.ds(0, ROWS - 1)], gram_recv.at[step, 0])
        gram[step, own_row] = jnp.sum(gram_got[step], axis=0)
        for peer in row_peers:
            mine = gram.at[step, own_row]
            remote(mine, mine, gram_send.at[step, 1], gram_recv.at[step, 1], (peer, col))
        right_got[step, row] = right_part[step, own_row]
        await_bytes(right_got.at[step, pl.ds(0, ROWS - 1)], right_recv.at[step, 0])
        right_sum[step, own_row] = jnp.sum(right_got[step], axis=0)
        for peer in row_peers:
            mine = right_sum.at[step, own_row]
            remote(mine, mine, right_send.at[step, 1], right_recv.at[step, 1], (peer, col))

        await_bytes(gram.at[step, pl.ds(0, RANK - 8)], gram_recv.at[step, 1])
        await_bytes(gram_got.at[step, pl.ds(0, ROWS - 1)], gram_send.at[step, 0])
        await_bytes(gram.at[step, pl.ds(0, RANK - 8)], gram_send.at[step, 1])
        inverse_factor(gram.at[step])
        await_bytes(right_sum.at[step, pl.ds(0, RANK - 8)], right_recv.at[step, 1])
        right[...] = contract(gram[step], right_sum[step], 1, 0)
        return carry

    lax.fori_loop(0, POWER, sweep, 0)
    last = POWER - 1

    square_own[...] = contract(jnp.ones((8, WIDE), jnp.float32), right[...] * right[...], 1, 1)[:1]
    square_got[col] = square_own[...]
    for peer in col_peers:
        remote(square_own, square_got.at[col], square_send, square_recv, (row, peer))
    left = contract(left_t[last], gram[last], 1, 1)
    moment_v[...] = blend[...] - DECAY_LEFT * contract(left, right[...], 1, 0)
    store = pltpu.make_async_copy(moment_v, new_momentum, out_sem.at[0])
    store.start()
    await_bytes(square_got.at[pl.ds(0, COLS - 1)], square_recv)
    norm = 1.0 / (jnp.sqrt(jnp.sum(square_got[...], axis=0)) + EPSILON)
    update_v[...] = contract(left * (norm * SCALE), right[...], 1, 0)
    store_update = pltpu.make_async_copy(update_v, update, out_sem.at[1])
    store_update.start()
    spot = lax.broadcasted_iota(jnp.int32, (RANK, RANK), 0) == lax.broadcasted_iota(jnp.int32, (RANK, RANK), 1)
    tall = jnp.sum(jnp.where(spot, jnp.broadcast_to(norm, (RANK, RANK)), 0.0), axis=1, keepdims=True)
    factor_v[...] = right[...] * tall
    store_factor = pltpu.make_async_copy(factor_v, new_factor, out_sem.at[2])
    store_factor.start()

    for step in range(POWER):
        await_bytes(left_got.at[step, pl.ds(0, COLS - 1)], left_send.at[step, 0])
        await_bytes(left_t.at[step, pl.ds(0, HIGH - 8)], left_send.at[step, 1])
        await_bytes(right_got.at[step, pl.ds(0, ROWS - 1)], right_send.at[step, 0])
        await_bytes(right_sum.at[step, pl.ds(0, RANK - 8)], right_send.at[step, 1])
    await_bytes(square_got.at[pl.ds(0, COLS - 1)], square_send)
    store.wait()
    store_update.wait()
    store_factor.wait()


def local(momentum, grads, right_factor):
    f32 = jnp.float32
    dma = pltpu.SemaphoreType.DMA
    return pl.pallas_call(
        kernel,
        out_shape=(
            jax.ShapeDtypeStruct((HIGH, WIDE), f32),
            jax.ShapeDtypeStruct((RANK, WIDE), f32),
            jax.ShapeDtypeStruct((HIGH, WIDE), f32),
        ),
        in_specs=[pl.BlockSpec(memory_space=pl.ANY)] * 3,
        out_specs=(pl.BlockSpec(memory_space=pl.ANY),) * 3,
        scratch_shapes=[
            pltpu.VMEM((HIGH, WIDE), f32),
            pltpu.VMEM((HIGH, WIDE), jnp.bfloat16),
            pltpu.VMEM((HIGH, WIDE), f32),
            pltpu.VMEM((RANK, WIDE), f32),
            pltpu.VMEM((POWER, HIGH, RANK), f32),
            pltpu.VMEM((POWER, COLS, 8, RANK), f32),
            pltpu.VMEM((POWER, HIGH, RANK), f32),
            pltpu.VMEM((POWER, RANK, RANK), f32),
            pltpu.VMEM((POWER, ROWS, 8, RANK), f32),
            pltpu.VMEM((POWER, RANK, RANK), f32),
            pltpu.VMEM((POWER, RANK, WIDE), f32),
            pltpu.VMEM((POWER, ROWS, 8, WIDE), f32),
            pltpu.VMEM((POWER, RANK, WIDE), f32),
            pltpu.VMEM((1, RANK), f32),
            pltpu.VMEM((COLS, 1, RANK), f32),
            pltpu.VMEM((RANK, WIDE), f32),
            pltpu.VMEM((HIGH, WIDE), f32),
            dma((3,)),
            dma((3,)),
            dma((POWER, 2)),
            dma((POWER, 2)),
            dma((POWER, 2)),
            dma((POWER, 2)),
            dma((POWER, 2)),
            dma((POWER, 2)),
            dma,
            dma,
        ],
        compiler_params=pltpu.CompilerParams(
            collective_id=0, has_side_effects=True, vmem_limit_bytes=16 << 20
        ),
    )(momentum, grads, right_factor)


def solution(mesh):
    return jax.shard_map(
        local,
        mesh=mesh,
        in_specs=(P("row", "col"), P(None, "row", "col"), P(None, "col")),
        out_specs=(P("row", "col"), P(None, "col"), P("row", "col")),
        check_vma=False,
    )
```

time: 1030 us -> 98.5 us (0.10)
  waiting for transfers between devices: 849 us -> 0 us
  blocking collectives: 97.8 us -> 0 us
  Pallas kernels: 0 us -> 93.5 us
  other arithmetic: 48.8 us -> 0 us
  between operations: 14.3 us -> 0.69 us
  matrix products: 13.5 us -> 0 us
    psum x6 -> x0, waiting for transfers between devices: 849 us -> none  [the longest x2 402 us: local(): left_t = lax.psum(partial_value, 'col')]
    psum x2 -> x0, blocking collectives: 97.8 us -> none  [local(): squares = lax.psum(jnp.sum(right_t * right_t, axis=1, keepdims=True), 'col')]
    pallas_call x0 -> x1, Pallas kernels: none -> 93.5 us  [local(): pl.pallas_call(kernel, out_shape=(jax.ShapeDtypeStruct((HIGH, WIDE), f32)...]
    another operation x10 -> x0, other arithmetic: 45.7 us -> none  [the longest x6 24.8 us: orthonormal(): lower_f = jnp.linalg.cholesky(gram_matrix)]
    dot_general x8 -> x0, matrix products: 12.9 us -> none  [contract(): lax.dot_general(first, second, (((first_dim,), (second_dim,)), ((), ())),...]
  transfers between devices with their start and end apart: 6 -> 0, of which waited for: 6 -> 0; matrix products, arithmetic and copies ran while one was open for 0% -> 0% of each run, Pallas kernels for 0% -> 0%
where the time goes in v1:
time: 98.5 us; the launch traced here: 98.4 us
  Pallas kernels  93.5 us (95%)
  local copies, waits for them, and re-layouts  4.2 us (4%)
    pallas_call x1, Pallas kernels, local(): pl.pallas_call(kernel, out_shape=(jax.ShapeDtypeStruct((HIGH, WIDE), f32)...  93.5 us
    pallas_call x3, local copies, waits for them, and re-layouts, local(): pl.pallas_call(kernel, out_shape=(jax.ShapeDtypeStruct((HIGH, WIDE), f32)...  2.73 us

profile of v1, /device:TPU:1, one launch (start us, length us, event | category | flops | bytes accessed | tf_op | source)
XLA Modules:
  0.0 98.4 jit_solution(9793651922050958941)
XLA Ops:
  0.6 0.0 copy-start.1
  0.6 0.0 copy-start
  0.7 1.1 %copy.7.grads = bf16[1,256,448]{2,1,0:T(8,128)(2,1)S(1)} copy(bf16[1,256,448]{1,2,0:T(8,128)(2,1)} %param.4) | data formatting | bytes 458752 | tf_op args[1]
  1.8 0.0 copy-done.1
  1.8 0.1 copy.8.factor_in
  1.9 0.0 copy-done
  2.0 0.2 copy.6.momentum
  2.2 93.5 %shard_map.58 = (f32[256,448]{1,0:T(8,128)S(1)}, f32[128,448]{1,0:T(8,128)S(1)}, f32[256,448]{1,0:T(8,128)S(1)}) custom-call(f32[256,448]{1,0:T(8,128)S(1)} %copy.6.momentum, bf16[1,256,448]{2,1,0:T(8,128)(2,1)S(1)} %copy.7.grads, f32[128,448]{1,0:T(8,128)S(1)} %copy.8.factor_in), custom_call_target="tpu_custom_call" | custom-call | tf_op jit(solution)/shard_map/pallas_call | solution.py:217
  95.7 1.0 copy.9
  96.6 0.8 copy.10
  97.4 1.0 copy.11
Async XLA Ops:
  0.6 1.2 %copy-start.1 = (f32[128,448]{0,1:T(8,128)S(1)}, f32[128,448]{0,1:T(8,128)}, u32[]{:S(2)}) copy-start(f32[128,448]{0,1:T(8,128)} %param.5) | copy-start | bytes 688132
  0.6 1.3 %copy-start = (f32[256,448]{0,1:T(8,128)S(1)}, f32[256,448]{0,1:T(8,128)}, u32[]{:S(2)}) copy-start(f32[256,448]{0,1:T(8,128)} %param.3) | copy-start | bytes 1376260

commit v2 on v1

v2 whole, which is shorter than its diff:
```python
import jax
import jax.numpy as jnp
from jax import lax
from jax.experimental import pallas as pl
from jax.experimental.pallas import tpu as pltpu
from jax.sharding import PartitionSpec as P

M = 4096
N = 14336
RANK = 128
POWER = 2

DECAY_LEFT = 0.05
EPSILON = 1e-06
SCALE = (M * N / RANK) ** 0.5

ROWS = 16
COLS = 32
HIGH = 256
WIDE = 448
SHARE = 32
OWNERS = WIDE // SHARE
GROUP = 8
MESH = pl.DeviceIdType.MESH

TURNS = sorted(
    ((dy, dx) for dy in range(4) for dx in range(4) if dy or dx),
    key=lambda turn: -(min(turn[0], 4 - turn[0]) + min(turn[1], 4 - turn[1])),
)


def contract(first, second, first_dim, second_dim):
    return lax.dot_general(
        first,
        second,
        (((first_dim,), (second_dim,)), ((), ())),
        precision=lax.Precision.HIGHEST,
        preferred_element_type=jnp.float32,
    )


def spread(x):
    return jnp.broadcast_to(x, (8, RANK))


def inverse_factor(w):
    lane = lax.broadcasted_iota(jnp.int32, (8, RANK), 1)
    sub = lax.broadcasted_iota(jnp.int32, (8, RANK), 0)
    count = RANK // 8
    tiles = [w[8 * i:8 * i + 8, :] for i in range(count)]
    for first in range(0, count, GROUP):
        stop = first + GROUP
        done, kept = [], []
        for k in range(first, stop):
            base = 8 * k
            tile = tiles[k]
            inside = (lane >= base) & (lane < base + 8)
            column = [spread(tile[:, base + t:base + t + 1]) for t in range(8)]
            d = {(i, t): spread(column[t][i:i + 1, :]) for t in range(8) for i in range(t, 8)}
            start = jnp.where(inside, jnp.where(lane - base == sub, 1.0, 0.0), tile)
            rows = [spread(start[i:i + 1, :]) for i in range(8)]
            low, scale = {}, []
            for t in range(8):
                inv = lax.rsqrt(d[t, t])
                scale.append(inv)
                for i in range(t + 1, 8):
                    low[i, t] = d[i, t] * inv
                rows[t] = rows[t] * inv
                for i in range(t + 1, 8):
                    for j in range(t + 1, i + 1):
                        d[i, j] = d[i, j] - low[i, t] * low[j, t]
                    rows[i] = rows[i] - low[i, t] * rows[t]
            block = rows[0]
            for t in range(1, 8):
                block = jnp.where(sub == t, rows[t], block)
            w[base:base + 8, :] = jnp.where(lane < base + 8, block, 0.0)
            done.append(block)
            kept.append(jnp.where((lane >= base + 8) & (lane < 8 * stop), 0.0, block))
            for kk in range(k + 1, stop):
                tile = tiles[kk]
                ls = []
                for t in range(8):
                    value = spread(tile[:, base + t:base + t + 1])
                    for s in range(t):
                        value = value - ls[s] * low[t, s]
                    ls.append(value * scale[t])
                tile = jnp.where(inside, 0.0, tile)
                for t in range(8):
                    tile = tile - ls[t] * rows[t]
                tiles[kk] = tile
        if stop < count:
            far = contract(jnp.concatenate(done, axis=0), jnp.concatenate(kept, axis=0), 0, 0)
            passed = (lane >= 8 * first) & (lane < 8 * stop)
            for kk in range(stop, count):
                tiles[kk] = jnp.where(passed, 0.0, tiles[kk]) - far[8 * kk:8 * kk + 8, :]


def kernel(
    momentum, grads, factor_in, moment_v, right, left_v, norm_v,
    grads_v, tall, blend, left_part, left_got, left_t,
    gram_part, gram_got, gram, right_part, right_got, right_sum,
    square_own, square_got, in_sem, left_send, left_recv, gram_send, gram_recv,
    right_send, right_recv, square_send, square_recv,
):
    row = lax.axis_index("row")
    col = lax.axis_index("col")
    y, x = row // 4, row % 4

    col_peers = [(col + 16 + (k + 1) // 2 * (1 if k % 2 else -1) + COLS) % COLS for k in range(31)]
    row_peers = [(y + dy) % 4 * 4 + (x + dx) % 4 for dy, dx in TURNS]

    barrier = pltpu.get_barrier_semaphore()
    for peer in col_peers:
        pl.semaphore_signal(barrier, inc=1, device_id=(row, peer), device_id_type=MESH)
    for peer in row_peers:
        pl.semaphore_signal(barrier, inc=1, device_id=(peer, col), device_id_type=MESH)

    loads = [
        pltpu.make_async_copy(momentum, moment_v, in_sem.at[1]),
        pltpu.make_async_copy(grads, grads_v, in_sem.at[2]),
        pltpu.make_async_copy(factor_in, right, in_sem.at[0]),
    ]
    for load in loads:
        load.start()
    for load in loads:
        load.wait()
    tall[...] = moment_v[...] + grads_v[...].astype(jnp.float32)
    blend[...] = tall[...].T

    def remote(src, dst, send, recv, device):
        pltpu.make_async_remote_copy(
            src_ref=src, dst_ref=dst, send_sem=send, recv_sem=recv,
            device_id=device, device_id_type=MESH,
        ).start()

    def await_bytes(ref, sem):
        pltpu.make_async_copy(ref, ref, sem).wait()

    own_col = pl.ds(pl.multiple_of(8 * col, 8), 8)
    own_row = pl.ds(pl.multiple_of(8 * row, 8), 8)

    def gathered(wait):
        @pl.when(row < OWNERS)
        def _():
            wait(WIDE - SHARE)

        @pl.when(row >= OWNERS)
        def _():
            wait(WIDE)

    def sweep(step, carry):
        left_part[step] = contract(blend[...], right[...], 1, 0)

        @pl.when(step == 0)
        def _():
            pl.semaphore_wait(barrier, 46)

        for peer in col_peers:
            part = left_part.at[step, pl.ds(pl.multiple_of(8 * peer, 8), 8)]
            remote(part, left_got.at[step, col], left_send.at[step, 0], left_recv.at[step, 0], (row, peer))
        left_got[step, col] = left_part[step, own_col]
        await_bytes(left_got.at[step, pl.ds(0, COLS - 1)], left_recv.at[step, 0])
        left_t[step, own_col] = jnp.sum(left_got[step], axis=0)
        for peer in col_peers:
            mine = left_t.at[step, own_col]
            remote(mine, mine, left_send.at[step, 1], left_recv.at[step, 1], (row, peer))
        await_bytes(left_t.at[step, pl.ds(0, HIGH - 8)], left_recv.at[step, 1])

        gram_part[step] = contract(left_t[step], left_t[step], 0, 0)
        for peer in row_peers:
            part = gram_part.at[step, pl.ds(pl.multiple_of(8 * peer, 8), 8)]
            remote(part, gram_got.at[step, row], gram_send.at[step, 0], gram_recv.at[step, 0], (peer, col))
        right_part[step] = contract(tall[...], left_t[step], 1, 0)
        for peer in row_peers:
            @pl.when(peer < OWNERS)
            def _():
                part = right_part.at[step, pl.ds(pl.multiple_of(SHARE * peer, SHARE), SHARE)]
                remote(part, right_got.at[step, row], right_send.at[step, 0], right_recv.at[step, 0], (peer, col))

        gram_got[step, row] = gram_part[step, own_row]
        await_bytes(gram_got.at[step, pl.ds(0, ROWS - 1)], gram_recv.at[step, 0])
        gram[step, own_row] = jnp.sum(gram_got[step], axis=0)
        for peer in row_peers:
            mine = gram.at[step, own_row]
            remote(mine, mine, gram_send.at[step, 1], gram_recv.at[step, 1], (peer, col))

        @pl.when(row < OWNERS)
        def _():
            share = pl.ds(pl.multiple_of(SHARE * row, SHARE), SHARE)
            right_got[step, row] = right_part[step, share]
            await_bytes(right_got.at[step, pl.ds(0, ROWS - 1)], right_recv.at[step, 0])
            right_sum[step, share] = jnp.sum(right_got[step], axis=0)
            for peer in row_peers:
                mine = right_sum.at[step, share]
                remote(mine, mine, right_send.at[step, 1], right_recv.at[step, 1], (peer, col))

        await_bytes(gram.at[step, pl.ds(0, RANK - 8)], gram_recv.at[step, 1])
        await_bytes(gram_got.at[step, pl.ds(0, ROWS - 1)], gram_send.at[step, 0])
        await_bytes(gram.at[step, pl.ds(0, RANK - 8)], gram_send.at[step, 1])
        inverse_factor(gram.at[step])
        gathered(lambda rows: await_bytes(right_sum.at[step, pl.ds(0, rows)], right_recv.at[step, 1]))
        right[...] = contract(right_sum[step], gram[step], 1, 1)
        return carry

    lax.fori_loop(0, POWER, sweep, 0)
    last = POWER - 1

    square_own[...] = jnp.sum(right[...] * right[...], axis=0, keepdims=True)
    square_got[col] = square_own[...]
    for peer in col_peers:
        remote(square_own, square_got.at[col], square_send, square_recv, (row, peer))
    left = contract(left_t[last], gram[last], 1, 1)
    moment_v[...] = tall[...] - DECAY_LEFT * contract(right[...], left, 1, 1)
    await_bytes(square_got.at[pl.ds(0, COLS - 1)], square_recv)
    norm = 1.0 / (jnp.sqrt(jnp.sum(square_got[...], axis=0)) + EPSILON)
    norm_v[...] = norm
    left_v[...] = left * (norm * SCALE)

    for step in range(POWER):
        await_bytes(left_got.at[step, pl.ds(0, COLS - 1)], left_send.at[step, 0])
        await_bytes(left_t.at[step, pl.ds(0, HIGH - 8)], left_send.at[step, 1])
        gathered(lambda rows: await_bytes(right_sum.at[step, pl.ds(0, rows)], right_send.at[step, 0]))

        @pl.when(row < OWNERS)
        def _():
            await_bytes(right_got.at[step, pl.ds(0, ROWS - 1)], right_send.at[step, 1])

    await_bytes(square_got.at[pl.ds(0, COLS - 1)], square_send)


def finish(moment, right, left, norm, new_momentum, new_factor, update, factor_v, update_v, out_sem):
    stores = [pltpu.make_async_copy(moment, new_momentum, out_sem.at[0])]
    stores[0].start()
    piece = WIDE // 4
    for k in range(4):
        rows = pl.ds(k * piece, piece)
        update_v[rows, :] = contract(right[rows, :], left[...], 1, 1)
        stores.append(pltpu.make_async_copy(update_v.at[rows], update.at[rows], out_sem.at[k + 1]))
        stores[-1].start()
    factor_v[...] = right[...] * norm[...]
    stores.append(pltpu.make_async_copy(factor_v, new_factor, out_sem.at[5]))
    stores[-1].start()
    for store in stores:
        store.wait()


def local(momentum, grads, right_factor):
    f32 = jnp.float32
    dma = pltpu.SemaphoreType.DMA
    passed = pl.pallas_call(
        kernel,
        out_shape=(
            jax.ShapeDtypeStruct((WIDE, HIGH), f32),
            jax.ShapeDtypeStruct((WIDE, RANK), f32),
            jax.ShapeDtypeStruct((HIGH, RANK), f32),
            jax.ShapeDtypeStruct((1, RANK), f32),
        ),
        in_specs=[pl.BlockSpec(memory_space=pltpu.HBM)] * 3,
        out_specs=(pl.BlockSpec(memory_space=pltpu.VMEM),) * 4,
        scratch_shapes=[
            pltpu.VMEM((WIDE, HIGH), jnp.bfloat16),
            pltpu.VMEM((WIDE, HIGH), f32),
            pltpu.VMEM((HIGH, WIDE), f32),
            pltpu.VMEM((POWER, HIGH, RANK), f32),
            pltpu.VMEM((POWER, COLS, 8, RANK), f32),
            pltpu.VMEM((POWER, HIGH, RANK), f32),
            pltpu.VMEM((POWER, RANK, RANK), f32),
            pltpu.VMEM((POWER, ROWS, 8, RANK), f32),
            pltpu.VMEM((POWER, RANK, RANK), f32),
            pltpu.VMEM((POWER, WIDE, RANK), f32),
            pltpu.VMEM((POWER, ROWS, SHARE, RANK), f32),
            pltpu.VMEM((POWER, WIDE, RANK), f32),
            pltpu.VMEM((1, RANK), f32),
            pltpu.VMEM((COLS, 1, RANK), f32),
            dma((3,)),
            dma((POWER, 2)),
            dma((POWER, 2)),
            dma((POWER, 2)),
            dma((POWER, 2)),
            dma((POWER, 2)),
            dma((POWER, 2)),
            dma,
            dma,
        ],
        compiler_params=pltpu.CompilerParams(
            collective_id=0, has_side_effects=True, vmem_limit_bytes=16 << 20
        ),
    )(*(pltpu.with_memory_space_constraint(given, pltpu.HBM) for given in (momentum.T, grads[0].T, right_factor.T)))
    outs = pl.pallas_call(
        finish,
        out_shape=(
            jax.ShapeDtypeStruct((WIDE, HIGH), f32),
            jax.ShapeDtypeStruct((WIDE, RANK), f32),
            jax.ShapeDtypeStruct((WIDE, HIGH), f32),
        ),
        in_specs=[pl.BlockSpec(memory_space=pltpu.VMEM)] * 4,
        out_specs=(pl.BlockSpec(memory_space=pltpu.HBM),) * 3,
        scratch_shapes=[pltpu.VMEM((WIDE, RANK), f32), pltpu.VMEM((WIDE, HIGH), f32), dma((6,))],
        compiler_params=pltpu.CompilerParams(vmem_limit_bytes=16 << 20),
    )(*passed)
    return tuple(out.T for out in outs)


def solution(mesh):
    return jax.shard_map(
        local,
        mesh=mesh,
        in_specs=(P("row", "col"), P(None, "row", "col"), P(None, "col")),
        out_specs=(P("row", "col"), P(None, "col"), P("row", "col")),
        check_vma=False,
    )
```

time: 98.5 us -> 92.3 us (0.937)
  local copies, waits for them, and re-layouts: 4.2 us -> 0 us
  Pallas kernels: 93.5 us -> 91.6 us
    pallas_call x3 -> x0, local copies, waits for them, and re-layouts: 2.73 us -> none  [local(): pl.pallas_call(kernel, out_shape=(jax.ShapeDtypeStruct((HIGH, WIDE), f32)...]
    pallas_call x1 -> x2, Pallas kernels: 93.5 us -> 91.6 us  [the longest x1 90.2 us: local(): pl.pallas_call(kernel, out_shape=(jax.ShapeDtypeStruct((WIDE, HIGH), f32)...]
    unnamed x7 -> x0, local copies, waits for them, and re-layouts: 1.47 us -> none
where the time goes in v2:
time: 92.3 us; the launch traced here: 92.2 us
  Pallas kernels  91.6 us (99%)
    pallas_call x1, Pallas kernels, local(): pl.pallas_call(kernel, out_shape=(jax.ShapeDtypeStruct((WIDE, HIGH), f32)...  90.2 us

profile of v2, /device:TPU:1, one launch (start us, length us, event | category | flops | bytes accessed | tf_op | source)
XLA Modules:
  0.0 92.2 jit_solution(15994985588879196029)
XLA Ops:
  0.6 90.2 %shard_map.58 = (f32[448,256]{1,0:T(8,128)S(1)}, f32[448,128]{1,0:T(8,128)S(1)}, f32[256,128]{1,0:T(8,128)S(1)}, f32[1,128]{1,0:T(1,128)S(1)}) custom-call(f32[448,256]{1,0:T(8,128)} %bitcast.8, bf16[448,256]{1,0:T(8,128)(2,1)} %bitcast.9, f32[448,128]{1,0:T(8,128)} %bitcast.10), custom_call_target="tpu_custom_call" | custom-call | tf_op jit(solution)/shard_map/pallas_call | solution.py:250
  90.8 1.4 %shard_map.59 = (f32[448,256]{1,0:T(8,128)}, f32[448,128]{1,0:T(8,128)}, f32[448,256]{1,0:T(8,128)}) custom-call(f32[448,256]{1,0:T(8,128)S(1)} %get-tuple-element.10.moment, f32[448,128]{1,0:T(8,128)S(1)} %get-tuple-element.11.right, f32[256,128]{1,0:T(8,128)S(1)} %get-tuple-element.12.left, f32[1,128]{1,0:T(1,128)S(1)} %get-tuple-element.13.norm), custom_call_target="tpu_custom_call" | custom-call | tf_op jit(solution)/shard_map/pallas_call | solution.py:289

commit v3 on v2

--- a/solution.py
+++ b/solution.py
@@ -16,12 +16,17 @@
 
 ROWS = 16
 COLS = 32
+CHIPS = 16
 HIGH = 256
+HALF = 128
+NEAR = 5
 WIDE = 448
 SHARE = 32
 OWNERS = WIDE // SHARE
 GROUP = 8
 MESH = pl.DeviceIdType.MESH
+
+HOPS = sorted((hop for hop in range(1 - CHIPS // 2, CHIPS // 2 + 1) if hop), key=lambda hop: -abs(hop))
 
 TURNS = sorted(
     ((dy, dx) for dy in range(4) for dx in range(4) if dy or dx),
@@ -97,16 +102,19 @@
 
 def kernel(
     momentum, grads, factor_in, moment_v, right, left_v, norm_v,
-    grads_v, tall, blend, left_part, left_got, left_t,
+    grads_v, tall, blend, half_out, half_own, half_got, left_part, left_got, left_t,
     gram_part, gram_got, gram, right_part, right_got, right_sum,
-    square_own, square_got, in_sem, left_send, left_recv, gram_send, gram_recv,
+    square_own, square_got, in_sem, pair_send, pair_recv, left_send, left_recv, gram_send, gram_recv,
     right_send, right_recv, square_send, square_recv,
 ):
     row = lax.axis_index("row")
     col = lax.axis_index("col")
     y, x = row // 4, row % 4
+    z, core = col // 2, col % 2
+    partner = (row, col + 1 - 2 * core)
 
     col_peers = [(col + 16 + (k + 1) // 2 * (1 if k % 2 else -1) + COLS) % COLS for k in range(31)]
+    chips = [(hop, (z + hop + CHIPS) % CHIPS) for hop in HOPS]
     row_peers = [(y + dy) % 4 * 4 + (x + dx) % 4 for dy, dx in TURNS]
 
     barrier = pltpu.get_barrier_semaphore()
@@ -136,7 +144,12 @@
     def await_bytes(ref, sem):
         pltpu.make_async_copy(ref, ref, sem).wait()
 
-    own_col = pl.ds(pl.multiple_of(8 * col, 8), 8)
+    ours = pl.multiple_of(HALF * core, HALF)
+    theirs = pl.multiple_of(HALF * (1 - core), HALF)
+
+    def piece(first, chip):
+        return pl.ds(pl.multiple_of(first + 8 * chip, 8), 8)
+
     own_row = pl.ds(pl.multiple_of(8 * row, 8), 8)
 
     def gathered(wait):
@@ -148,23 +161,44 @@
         def _():
             wait(WIDE)
 
+    last = POWER - 1
+
     def sweep(step, carry):
-        left_part[step] = contract(blend[...], right[...], 1, 0)
+        half_out[step] = contract(blend[pl.ds(theirs, HALF), :], right[...], 1, 0)
 
         @pl.when(step == 0)
         def _():
             pl.semaphore_wait(barrier, 46)
 
-        for peer in col_peers:
-            part = left_part.at[step, pl.ds(pl.multiple_of(8 * peer, 8), 8)]
-            remote(part, left_got.at[step, col], left_send.at[step, 0], left_recv.at[step, 0], (row, peer))
-        left_got[step, col] = left_part[step, own_col]
-        await_bytes(left_got.at[step, pl.ds(0, COLS - 1)], left_recv.at[step, 0])
-        left_t[step, own_col] = jnp.sum(left_got[step], axis=0)
-        for peer in col_peers:
-            mine = left_t.at[step, own_col]
-            remote(mine, mine, left_send.at[step, 1], left_recv.at[step, 1], (row, peer))
-        await_bytes(left_t.at[step, pl.ds(0, HIGH - 8)], left_recv.at[step, 1])
+        remote(half_out.at[step], half_got.at[step], pair_send.at[step, 0], pair_recv.at[step, 0], partner)
+        half_own[...] = contract(blend[pl.ds(ours, HALF), :], right[...], 1, 0)
+        await_bytes(half_got.at[step], pair_recv.at[step, 0])
+        left_part[step] = half_own[...] + half_got[step]
+        for hop, chip in chips:
+            part = left_part.at[step, piece(0, chip)]
+            remote(part, left_got.at[step, z], left_send.at[step, 0], left_recv.at[step, 0], (row, 2 * chip + core))
+        left_got[step, z] = left_part[step, piece(0, z)]
+        await_bytes(left_got.at[step, pl.ds(0, CHIPS - 1)], left_recv.at[step, 0])
+        left_t[step, piece(ours, z)] = jnp.sum(left_got[step], axis=0)
+        mine = left_t.at[step, piece(ours, z)]
+        for hop, chip in chips:
+            arrival = left_recv.at[step, 1 if abs(hop) <= NEAR else 2]
+            remote(mine, mine, left_send.at[step, 1], arrival, (row, 2 * chip + core))
+
+        def forward(chip):
+            part = left_t.at[step, piece(ours, chip)]
+            remote(part, part, pair_send.at[step, 1], pair_recv.at[step, 1], partner)
+
+        forward(z)
+        near = [chip for hop, chip in chips if abs(hop) <= NEAR]
+        far = [chip for hop, chip in chips if abs(hop) > NEAR]
+        await_bytes(left_t.at[step, pl.ds(0, 8 * len(near))], left_recv.at[step, 1])
+        for chip in near:
+            forward(chip)
+        await_bytes(left_t.at[step, pl.ds(0, 8 * len(far))], left_recv.at[step, 2])
+        for chip in far:
+            forward(chip)
+        await_bytes(left_t.at[step, pl.ds(0, HALF)], pair_recv.at[step, 1])
 
         gram_part[step] = contract(left_t[step], left_t[step], 0, 0)
         for peer in row_peers:
@@ -199,12 +233,12 @@
         await_bytes(gram.at[step, pl.ds(0, RANK - 8)], gram_send.at[step, 1])
         inverse_factor(gram.at[step])
         gathered(lambda rows: await_bytes(right_sum.at[step, pl.ds(0, rows)], right_recv.at[step, 1]))
-        right[...] = contract(right_sum[step], gram[step], 1, 1)
+        spot = lax.broadcasted_iota(jnp.int32, (RANK, RANK), 0) == lax.broadcasted_iota(jnp.int32, (RANK, RANK), 1)
+        weight = jnp.sqrt(jnp.sum(jnp.where(spot, gram[step], 0.0), axis=0, keepdims=True))
+        right[...] = contract(right_sum[step], gram[step], 1, 1) * jnp.where(step < last, weight, 1.0)
         return carry
 
     lax.fori_loop(0, POWER, sweep, 0)
-    last = POWER - 1
-
     square_own[...] = jnp.sum(right[...] * right[...], axis=0, keepdims=True)
     square_got[col] = square_own[...]
     for peer in col_peers:
@@ -217,8 +251,10 @@
     left_v[...] = left * (norm * SCALE)
 
     for step in range(POWER):
-        await_bytes(left_got.at[step, pl.ds(0, COLS - 1)], left_send.at[step, 0])
-        await_bytes(left_t.at[step, pl.ds(0, HIGH - 8)], left_send.at[step, 1])
+        await_bytes(half_got.at[step], pair_send.at[step, 0])
+        await_bytes(left_t.at[step, pl.ds(0, HALF)], pair_send.at[step, 1])
+        await_bytes(left_got.at[step, pl.ds(0, CHIPS - 1)], left_send.at[step, 0])
+        await_bytes(left_t.at[step, pl.ds(0, HALF - 8)], left_send.at[step, 1])
         gathered(lambda rows: await_bytes(right_sum.at[step, pl.ds(0, rows)], right_send.at[step, 0]))
 
         @pl.when(row < OWNERS)
@@ -261,8 +297,11 @@
             pltpu.VMEM((WIDE, HIGH), jnp.bfloat16),
             pltpu.VMEM((WIDE, HIGH), f32),
             pltpu.VMEM((HIGH, WIDE), f32),
-            pltpu.VMEM((POWER, HIGH, RANK), f32),
-            pltpu.VMEM((POWER, COLS, 8, RANK), f32),
+            pltpu.VMEM((POWER, HALF, RANK), f32),
+            pltpu.VMEM((HALF, RANK), f32),
+            pltpu.VMEM((POWER, HALF, RANK), f32),
+            pltpu.VMEM((POWER, HALF, RANK), f32),
+            pltpu.VMEM((POWER, CHIPS, 8, RANK), f32),
             pltpu.VMEM((POWER, HIGH, RANK), f32),
             pltpu.VMEM((POWER, RANK, RANK), f32),
             pltpu.VMEM((POWER, ROWS, 8, RANK), f32),
@@ -275,6 +314,8 @@
             dma((3,)),
             dma((POWER, 2)),
             dma((POWER, 2)),
+            dma((POWER, 2)),
+            dma((POWER, 3)),
             dma((POWER, 2)),
             dma((POWER, 2)),
             dma((POWER, 2)),

time: 92.3 us -> 86 us (0.932)
  Pallas kernels: 91.6 us -> 85.2 us
    pallas_call x1, Pallas kernels: 90.2 us -> 83.8 us  [local(): pl.pallas_call(kernel, out_shape=(jax.ShapeDtypeStruct((WIDE, HIGH), f32)...]
where the time goes in v3:
time: 86 us; the launch traced here: 85.9 us
  Pallas kernels  85.2 us (99%)
    pallas_call x1, Pallas kernels, local(): pl.pallas_call(kernel, out_shape=(jax.ShapeDtypeStruct((WIDE, HIGH), f32)...  83.8 us

profile of v3, /device:TPU:1, one launch (start us, length us, event | category | flops | bytes accessed | tf_op | source)
XLA Modules:
  0.0 85.9 jit_solution(17930220350832913175)
XLA Ops:
  0.6 83.8 %shard_map.58 = (f32[448,256]{1,0:T(8,128)S(1)}, f32[448,128]{1,0:T(8,128)S(1)}, f32[256,128]{1,0:T(8,128)S(1)}, f32[1,128]{1,0:T(1,128)S(1)}) custom-call(f32[448,256]{1,0:T(8,128)} %bitcast.8, bf16[448,256]{1,0:T(8,128)(2,1)} %bitcast.9, f32[448,128]{1,0:T(8,128)} %bitcast.10), custom_call_target="tpu_custom_call" | custom-call | tf_op jit(solution)/shard_map/pallas_call | solution.py:286
  84.5 1.4 %shard_map.59 = (f32[448,256]{1,0:T(8,128)}, f32[448,128]{1,0:T(8,128)}, f32[448,256]{1,0:T(8,128)}) custom-call(f32[448,256]{1,0:T(8,128)S(1)} %get-tuple-element.10.moment, f32[448,128]{1,0:T(8,128)S(1)} %get-tuple-element.11.right, f32[256,128]{1,0:T(8,128)S(1)} %get-tuple-element.12.left, f32[1,128]{1,0:T(1,128)S(1)} %get-tuple-element.13.norm), custom_call_target="tpu_custom_call" | custom-call | tf_op jit(solution)/shard_map/pallas_call | solution.py:330

commit v4 on v3

v4 whole, which is shorter than its diff:
```python
import jax
import jax.numpy as jnp
from jax import lax
from jax.experimental import pallas as pl
from jax.experimental.pallas import tpu as pltpu
from jax.sharding import PartitionSpec as P

M = 4096
N = 14336
RANK = 128
POWER = 2

DECAY_LEFT = 0.05
EPSILON = 1e-06
SCALE = (M * N / RANK) ** 0.5

ROWS = 16
COLS = 32
CHIPS = 16
HIGH = 256
HALF = 128
NEAR = 5
WIDE = 448
GROUP = 8
MESH = pl.DeviceIdType.MESH

HOPS = sorted((hop for hop in range(1 - CHIPS // 2, CHIPS // 2 + 1) if hop), key=lambda hop: -abs(hop))

TURNS = sorted(
    ((dy, dx) for dy in range(4) for dx in range(4) if dy or dx),
    key=lambda turn: -(min(turn[0], 4 - turn[0]) + min(turn[1], 4 - turn[1])),
)


def contract(first, second, first_dim, second_dim):
    return lax.dot_general(
        first,
        second,
        (((first_dim,), (second_dim,)), ((), ())),
        precision=lax.Precision.HIGHEST,
        preferred_element_type=jnp.float32,
    )


def spread(x):
    return jnp.broadcast_to(x, (8, RANK))


def inverse_factor(w, plain):
    lane = lax.broadcasted_iota(jnp.int32, (8, RANK), 1)
    sub = lax.broadcasted_iota(jnp.int32, (8, RANK), 0)
    count = RANK // 8
    tiles = [w[8 * i:8 * i + 8, :] for i in range(count)]
    for first in range(0, count, GROUP):
        stop = first + GROUP
        done, kept = [], []
        for k in range(first, stop):
            base = 8 * k
            tile = tiles[k]
            inside = (lane >= base) & (lane < base + 8)
            column = [jnp.where(sub >= 0, spread(tile[:, base + t:base + t + 1]), 0.0) for t in range(8)]
            d = {(i, t): spread(column[t][i:i + 1, :]) for t in range(8) for i in range(t, 8)}
            start = jnp.where(inside, jnp.where(lane - base == sub, 1.0, 0.0), tile)
            rows = [spread(start[i:i + 1, :]) for i in range(8)]
            low, scale = {}, []
            for t in range(8):
                inv = lax.rsqrt(d[t, t])
                scale.append(inv)
                for i in range(t + 1, 8):
                    low[i, t] = d[i, t] * inv
                rows[t] = rows[t] * inv
                for i in range(t + 1, 8):
                    for j in range(t + 1, i + 1):
                        d[i, j] = d[i, j] - low[i, t] * low[j, t]
                    rows[i] = rows[i] - low[i, t] * rows[t]
            block, factor = rows[0], scale[0]
            for t in range(1, 8):
                block = jnp.where(sub == t, rows[t], block)
                factor = jnp.where(sub == t, scale[t], factor)
            factor = jnp.where(plain, 1.0, jnp.sqrt(factor))
            w[base:base + 8, :] = jnp.where(lane < base + 8, block * factor, 0.0)
            done.append(block)
            kept.append(jnp.where((lane >= base + 8) & (lane < 8 * stop), 0.0, block))
            for kk in range(k + 1, stop):
                tile = tiles[kk]
                ls = []
                for t in range(8):
                    value = spread(tile[:, base + t:base + t + 1])
                    for s in range(t):
                        value = value - ls[s] * low[t, s]
                    ls.append(value * scale[t])
                tile = jnp.where(inside, 0.0, tile)
                for t in range(8):
                    tile = tile - ls[t] * rows[t]
                tiles[kk] = tile
        if stop < count:
            far = contract(jnp.concatenate(done, axis=0), jnp.concatenate(kept, axis=0), 0, 0)
            passed = (lane >= 8 * first) & (lane < 8 * stop)
            for kk in range(stop, count):
                tiles[kk] = jnp.where(passed, 0.0, tiles[kk]) - far[8 * kk:8 * kk + 8, :]


def kernel(
    momentum, grads, factor_in, moment, right_tall, left, norm,
    momentum_v, grads_v, factor_v, tall, blend, right,
    half_out, half_own, half_got, left_part, left_got, left_h,
    gram_part, gram_got, gram, right_part, right_got, right_sum, square_own, square_got,
    in_sem, pair_send, pair_recv, left_send, left_recv, gram_send, gram_recv,
    right_send, right_recv, square_send, square_recv,
):
    row = lax.axis_index("row")
    col = lax.axis_index("col")
    y, x = row // 4, row % 4
    z, core = col // 2, col % 2
    partner = (row, col + 1 - 2 * core)

    col_peers = [(col + 16 + (k + 1) // 2 * (1 if k % 2 else -1) + COLS) % COLS for k in range(31)]
    chips = [(hop, (z + hop + CHIPS) % CHIPS) for hop in HOPS]
    row_peers = [(y + dy) % 4 * 4 + (x + dx) % 4 for dy, dx in TURNS]

    barrier = pltpu.get_barrier_semaphore()
    for peer in col_peers:
        pl.semaphore_signal(barrier, inc=1, device_id=(row, peer), device_id_type=MESH)
    for peer in row_peers:
        pl.semaphore_signal(barrier, inc=1, device_id=(peer, col), device_id_type=MESH)

    loads = [
        pltpu.make_async_copy(momentum, momentum_v, in_sem.at[0]),
        pltpu.make_async_copy(grads, grads_v, in_sem.at[1]),
        pltpu.make_async_copy(factor_in, factor_v, in_sem.at[2]),
    ]
    for load in loads:
        load.start()
    for load in loads:
        load.wait()
    tall[...] = momentum_v[...] + grads_v[...].astype(jnp.float32)
    blend[...] = tall[...].T
    right[...] = factor_v[...].T

    def remote(src, dst, send, recv, device):
        pltpu.make_async_remote_copy(
            src_ref=src, dst_ref=dst, send_sem=send, recv_sem=recv,
            device_id=device, device_id_type=MESH,
        ).start()

    def await_bytes(ref, sem):
        pltpu.make_async_copy(ref, ref, sem).wait()

    def piece(place):
        return pl.ds(pl.multiple_of(8 * place, 8), 8)

    last = POWER - 1

    def sweep(step, carry):
        part = contract(right[...], tall[...], 1, 0)
        first, second = part[:, :HALF], part[:, HALF:]
        half_out[step] = jnp.where(core == 0, second, first)
        half_own[...] = jnp.where(core == 0, first, second)

        @pl.when(step == 0)
        def _():
            pl.semaphore_wait(barrier, 46)

        remote(half_out.at[step], half_got.at[step], pair_send.at[step, 0], pair_recv.at[step, 0], partner)
        await_bytes(half_got.at[step], pair_recv.at[step, 0])
        left_part[step] = half_own[...] + half_got[step]
        for hop, chip in chips:
            share = left_part.at[step, piece(chip)]
            remote(share, left_got.at[step, z], left_send.at[step, 0], left_recv.at[step, 0], (row, 2 * chip + core))
        left_got[step, z] = left_part[step, piece(z)]
        await_bytes(left_got.at[step, pl.ds(0, CHIPS - 1)], left_recv.at[step, 0])
        left_h[step, core, piece(z)] = jnp.sum(left_got[step], axis=0)
        mine = left_h.at[step, core, piece(z)]
        for hop, chip in chips:
            arrival = left_recv.at[step, 1 if abs(hop) <= NEAR else 2]
            remote(mine, mine, left_send.at[step, 1], arrival, (row, 2 * chip + core))

        def forward(chip):
            share = left_h.at[step, core, piece(chip)]
            remote(share, share, pair_send.at[step, 1], pair_recv.at[step, 1], partner)

        forward(z)
        near = [chip for hop, chip in chips if abs(hop) <= NEAR]
        far = [chip for hop, chip in chips if abs(hop) > NEAR]
        await_bytes(left_part.at[step, pl.ds(0, 8 * len(near))], left_recv.at[step, 1])
        for chip in near:
            forward(chip)
        await_bytes(left_part.at[step, pl.ds(0, 8 * len(far))], left_recv.at[step, 2])
        for chip in far:
            forward(chip)
        await_bytes(left_part.at[step], pair_recv.at[step, 1])

        raw = jnp.concatenate([left_h[step, 0], left_h[step, 1]], axis=1)
        gram_part[step] = contract(raw, raw, 1, 1)
        for peer in row_peers:
            share = gram_part.at[step, piece(peer)]
            remote(share, gram_got.at[step, row], gram_send.at[step, 0], gram_recv.at[step, 0], (peer, col))
        right_part[step] = contract(raw, blend[...], 1, 0)
        for peer in row_peers:
            share = right_part.at[step, piece(peer)]
            remote(share, right_got.at[step, row], right_send.at[step, 0], right_recv.at[step, 0], (peer, col))

        gram_got[step, row] = gram_part[step, piece(row)]
        await_bytes(gram_got.at[step, pl.ds(0, ROWS - 1)], gram_recv.at[step, 0])
        gram[step, piece(row)] = jnp.sum(gram_got[step], axis=0)
        for peer in row_peers:
            share = gram.at[step, piece(row)]
            remote(share, share, gram_send.at[step, 1], gram_recv.at[step, 1], (peer, col))
        right_got[step, row] = right_part[step, piece(row)]
        await_bytes(right_got.at[step, pl.ds(0, ROWS - 1)], right_recv.at[step, 0])
        right_sum[step, piece(row)] = jnp.sum(right_got[step], axis=0)
        for peer in row_peers:
            share = right_sum.at[step, piece(row)]
            remote(share, share, right_send.at[step, 1], right_recv.at[step, 1], (peer, col))

        await_bytes(gram.at[step, pl.ds(0, RANK - 8)], gram_recv.at[step, 1])
        await_bytes(gram_got.at[step, pl.ds(0, ROWS - 1)], gram_send.at[step, 0])
        await_bytes(gram.at[step, pl.ds(0, RANK - 8)], gram_send.at[step, 1])
        inverse_factor(gram.at[step], step == last)
        await_bytes(right_sum.at[step, pl.ds(0, RANK - 8)], right_recv.at[step, 1])
        right[...] = contract(gram[step], right_sum[step], 1, 0)
        return carry

    lax.fori_loop(0, POWER, sweep, 0)

    right_tall[...] = right[...].T
    square_own[...] = jnp.sum(right_tall[...] * right_tall[...], axis=0, keepdims=True)
    square_got[col] = square_own[...]
    for peer in col_peers:
        remote(square_own, square_got.at[col], square_send, square_recv, (row, peer))
    left[:, :HALF] = contract(gram[last], left_h[last, 0], 1, 0)
    left[:, HALF:] = contract(gram[last], left_h[last, 1], 1, 0)
    moment[...] = tall[...] - DECAY_LEFT * contract(right_tall[...], left[...], 1, 0)
    await_bytes(square_got.at[pl.ds(0, COLS - 1)], square_recv)
    norm[...] = 1.0 / (jnp.sqrt(jnp.sum(square_got[...], axis=0)) + EPSILON)

    for step in range(POWER):
        await_bytes(half_got.at[step], pair_send.at[step, 0])
        await_bytes(left_part.at[step], pair_send.at[step, 1])
        await_bytes(left_got.at[step, pl.ds(0, CHIPS - 1)], left_send.at[step, 0])
        await_bytes(left_part.at[step, pl.ds(0, HALF - 8)], left_send.at[step, 1])
        await_bytes(right_got.at[step, pl.ds(0, ROWS - 1)], right_send.at[step, 0])
        await_bytes(right_sum.at[step, pl.ds(0, RANK - 8)], right_send.at[step, 1])
    await_bytes(square_got.at[pl.ds(0, COLS - 1)], square_send)


def finish(moment, right_tall, left, norm, new_momentum, new_factor, update, factor_v, update_v, out_sem):
    stores = [pltpu.make_async_copy(moment, new_momentum, out_sem.at[0])]
    stores[0].start()
    factor_v[...] = right_tall[...] * norm[...]
    stores.append(pltpu.make_async_copy(factor_v, new_factor, out_sem.at[1]))
    stores[-1].start()
    span = WIDE // 4
    for k in range(4):
        rows = pl.ds(k * span, span)
        update_v[rows, :] = contract(factor_v[rows, :] * SCALE, left[...], 1, 0)
        stores.append(pltpu.make_async_copy(update_v.at[rows], update.at[rows], out_sem.at[k + 2]))
        stores[-1].start()
    for store in stores:
        store.wait()


def local(momentum, grads, right_factor):
    f32 = jnp.float32
    dma = pltpu.SemaphoreType.DMA
    given = (momentum.T, grads[0].T, right_factor.T)
    passed = pl.pallas_call(
        kernel,
        out_shape=(
            jax.ShapeDtypeStruct((WIDE, HIGH), f32),
            jax.ShapeDtypeStruct((WIDE, RANK), f32),
            jax.ShapeDtypeStruct((RANK, HIGH), f32),
            jax.ShapeDtypeStruct((1, RANK), f32),
        ),
        in_specs=[pl.BlockSpec(memory_space=pltpu.HBM)] * 3,
        out_specs=(pl.BlockSpec(memory_space=pltpu.VMEM),) * 4,
        scratch_shapes=[
            pltpu.VMEM((WIDE, HIGH), f32),
            pltpu.VMEM((WIDE, HIGH), jnp.bfloat16),
            pltpu.VMEM((WIDE, RANK), f32),
            pltpu.VMEM((WIDE, HIGH), f32),
            pltpu.VMEM((HIGH, WIDE), f32),
            pltpu.VMEM((RANK, WIDE), f32),
            pltpu.VMEM((POWER, RANK, HALF), f32),
            pltpu.VMEM((RANK, HALF), f32),
            pltpu.VMEM((POWER, RANK, HALF), f32),
            pltpu.VMEM((POWER, RANK, HALF), f32),
            pltpu.VMEM((POWER, CHIPS, 8, HALF), f32),
            pltpu.VMEM((POWER, 2, RANK, HALF), f32),
            pltpu.VMEM((POWER, RANK, RANK), f32),
            pltpu.VMEM((POWER, ROWS, 8, RANK), f32),
            pltpu.VMEM((POWER, RANK, RANK), f32),
            pltpu.VMEM((POWER, RANK, WIDE), f32),
            pltpu.VMEM((POWER, ROWS, 8, WIDE), f32),
            pltpu.VMEM((POWER, RANK, WIDE), f32),
            pltpu.VMEM((1, RANK), f32),
            pltpu.VMEM((COLS, 1, RANK), f32),
            dma((3,)),
            dma((POWER, 2)),
            dma((POWER, 2)),
            dma((POWER, 2)),
            dma((POWER, 3)),
            dma((POWER, 2)),
            dma((POWER, 2)),
            dma((POWER, 2)),
            dma((POWER, 2)),
            dma,
            dma,
        ],
        compiler_params=pltpu.CompilerParams(
            collective_id=0, has_side_effects=True, vmem_limit_bytes=16 << 20
        ),
    )(*(pltpu.with_memory_space_constraint(array, pltpu.HBM) for array in given))
    outs = pl.pallas_call(
        finish,
        out_shape=(
            jax.ShapeDtypeStruct((WIDE, HIGH), f32),
            jax.ShapeDtypeStruct((WIDE, RANK), f32),
            jax.ShapeDtypeStruct((WIDE, HIGH), f32),
        ),
        in_specs=[pl.BlockSpec(memory_space=pltpu.VMEM)] * 4,
        out_specs=(pl.BlockSpec(memory_space=pltpu.HBM),) * 3,
        scratch_shapes=[pltpu.VMEM((WIDE, RANK), f32), pltpu.VMEM((WIDE, HIGH), f32), dma((6,))],
        compiler_params=pltpu.CompilerParams(vmem_limit_bytes=16 << 20),
    )(*passed)
    return tuple(out.T for out in outs)


def solution(mesh):
    return jax.shard_map(
        local,
        mesh=mesh,
        in_specs=(P("row", "col"), P(None, "row", "col"), P(None, "col")),
        out_specs=(P("row", "col"), P(None, "col"), P("row", "col")),
        check_vma=False,
    )
```

time: 86 us -> 85.3 us (level)
  no operation moved by 1% of the time
where the time goes in v4:
time: 85.3 us; the launch traced here: 85.1 us
  Pallas kernels  84.5 us (99%)
    pallas_call x1, Pallas kernels, local(): pl.pallas_call(kernel, out_shape=(jax.ShapeDtypeStruct((WIDE, HIGH), f32)...  83.2 us

profile of v4, /device:TPU:1, one launch (start us, length us, event | category | flops | bytes accessed | tf_op | source)
XLA Modules:
  0.0 85.1 jit_solution(9368367286161087249)
XLA Ops:
  0.6 83.2 %shard_map.58 = (f32[448,256]{1,0:T(8,128)S(1)}, f32[448,128]{1,0:T(8,128)S(1)}, f32[128,256]{1,0:T(8,128)S(1)}, f32[1,128]{1,0:T(1,128)S(1)}) custom-call(f32[448,256]{1,0:T(8,128)} %bitcast.8, bf16[448,256]{1,0:T(8,128)(2,1)} %bitcast.9, f32[448,128]{1,0:T(8,128)} %bitcast.10), custom_call_target="tpu_custom_call" | custom-call | tf_op jit(solution)/shard_map/pallas_call | solution.py:267
  83.9 1.2 %shard_map.59 = (f32[448,256]{1,0:T(8,128)}, f32[448,128]{1,0:T(8,128)}, f32[448,256]{1,0:T(8,128)}) custom-call(f32[448,256]{1,0:T(8,128)S(1)} %get-tuple-element.10.moment, f32[448,128]{1,0:T(8,128)S(1)} %get-tuple-element.11.right_tall, f32[128,256]{1,0:T(8,128)S(1)} %get-tuple-element.12.left, f32[1,128]{1,0:T(1,128)S(1)} %get-tuple-element.13.norm), custom_call_target="tpu_custom_call" | custom-call | tf_op jit(solution)/shard_map/pallas_call | solution.py:314

commit v5 on v4

--- a/solution.py
+++ b/solution.py
@@ -123,6 +123,8 @@
         pl.semaphore_signal(barrier, inc=1, device_id=(row, peer), device_id_type=MESH)
     for peer in row_peers:
         pl.semaphore_signal(barrier, inc=1, device_id=(peer, col), device_id_type=MESH)
+    for peer in row_peers:
+        pl.semaphore_signal(barrier, inc=1, device_id=(peer, partner[1]), device_id_type=MESH)
 
     loads = [
         pltpu.make_async_copy(momentum, momentum_v, in_sem.at[0]),
@@ -134,7 +136,6 @@
     for load in loads:
         load.wait()
     tall[...] = momentum_v[...] + grads_v[...].astype(jnp.float32)
-    blend[...] = tall[...].T
     right[...] = factor_v[...].T
 
     def remote(src, dst, send, recv, device):
@@ -149,6 +150,7 @@
     def piece(place):
         return pl.ds(pl.multiple_of(8 * place, 8), 8)
 
+    owner = row % 2 == core
     last = POWER - 1
 
     def sweep(step, carry):
@@ -159,7 +161,7 @@
 
         @pl.when(step == 0)
         def _():
-            pl.semaphore_wait(barrier, 46)
+            pl.semaphore_wait(barrier, 61)
 
         remote(half_out.at[step], half_got.at[step], pair_send.at[step, 0], pair_recv.at[step, 0], partner)
         await_bytes(half_got.at[step], pair_recv.at[step, 0])
@@ -168,6 +170,11 @@
             share = left_part.at[step, piece(chip)]
             remote(share, left_got.at[step, z], left_send.at[step, 0], left_recv.at[step, 0], (row, 2 * chip + core))
         left_got[step, z] = left_part[step, piece(z)]
+
+        @pl.when(step == 0)
+        def _():
+            blend[...] = tall[...].T
+
         await_bytes(left_got.at[step, pl.ds(0, CHIPS - 1)], left_recv.at[step, 0])
         left_h[step, core, piece(z)] = jnp.sum(left_got[step], axis=0)
         mine = left_h.at[step, core, piece(z)]
@@ -193,19 +200,27 @@
         raw = jnp.concatenate([left_h[step, 0], left_h[step, 1]], axis=1)
         gram_part[step] = contract(raw, raw, 1, 1)
         for peer in row_peers:
-            share = gram_part.at[step, piece(peer)]
-            remote(share, gram_got.at[step, row], gram_send.at[step, 0], gram_recv.at[step, 0], (peer, col))
+            @pl.when(peer % 2 == core)
+            def _():
+                share = gram_part.at[step, piece(peer)]
+                remote(share, gram_got.at[step, row], gram_send.at[step, 0], gram_recv.at[step, 0], (peer, col))
+
         right_part[step] = contract(raw, blend[...], 1, 0)
         for peer in row_peers:
             share = right_part.at[step, piece(peer)]
             remote(share, right_got.at[step, row], right_send.at[step, 0], right_recv.at[step, 0], (peer, col))
 
-        gram_got[step, row] = gram_part[step, piece(row)]
-        await_bytes(gram_got.at[step, pl.ds(0, ROWS - 1)], gram_recv.at[step, 0])
-        gram[step, piece(row)] = jnp.sum(gram_got[step], axis=0)
-        for peer in row_peers:
+        @pl.when(owner)
+        def _():
+            gram_got[step, row] = gram_part[step, piece(row)]
+            await_bytes(gram_got.at[step, pl.ds(0, ROWS - 1)], gram_recv.at[step, 0])
+            gram[step, piece(row)] = jnp.sum(gram_got[step], axis=0)
             share = gram.at[step, piece(row)]
-            remote(share, share, gram_send.at[step, 1], gram_recv.at[step, 1], (peer, col))
+            for peer in row_peers:
+                for side in (col, partner[1]):
+                    remote(share, share, gram_send.at[step, 1], gram_recv.at[step, 1], (peer, side))
+            remote(share, share, gram_send.at[step, 1], gram_recv.at[step, 1], partner)
+
         right_got[step, row] = right_part[step, piece(row)]
         await_bytes(right_got.at[step, pl.ds(0, ROWS - 1)], right_recv.at[step, 0])
         right_sum[step, piece(row)] = jnp.sum(right_got[step], axis=0)
@@ -213,9 +228,19 @@
             share = right_sum.at[step, piece(row)]
             remote(share, share, right_send.at[step, 1], right_recv.at[step, 1], (peer, col))
 
-        await_bytes(gram.at[step, pl.ds(0, RANK - 8)], gram_recv.at[step, 1])
-        await_bytes(gram_got.at[step, pl.ds(0, ROWS - 1)], gram_send.at[step, 0])
-        await_bytes(gram.at[step, pl.ds(0, RANK - 8)], gram_send.at[step, 1])
+        @pl.when(owner)
+        def _():
+            await_bytes(gram.at[step, pl.ds(0, RANK - 8)], gram_recv.at[step, 1])
+            await_bytes(gram_got.at[step, pl.ds(0, ROWS // 2 - 1)], gram_send.at[step, 0])
+            for side in range(2):
+                await_bytes(gram_got.at[step, pl.ds(0, ROWS - 1)], gram_send.at[step, 1])
+            await_bytes(gram_got.at[step, 0], gram_send.at[step, 1])
+
+        @pl.when(jnp.logical_not(owner))
+        def _():
+            await_bytes(gram.at[step], gram_recv.at[step, 1])
+            await_bytes(gram_got.at[step, pl.ds(0, ROWS // 2)], gram_send.at[step, 0])
+
         inverse_factor(gram.at[step], step == last)
         await_bytes(right_sum.at[step, pl.ds(0, RANK - 8)], right_recv.at[step, 1])
         right[...] = contract(gram[step], right_sum[step], 1, 0)

time: 85.3 us -> 84.9 us (level)
  no operation moved by 1% of the time
where the time goes in v5:
time: 84.9 us; the launch traced here: 84.8 us
  Pallas kernels  84.1 us (99%)
    pallas_call x1, Pallas kernels, local(): pl.pallas_call(kernel, out_shape=(jax.ShapeDtypeStruct((WIDE, HIGH), f32)...  82.9 us

profile of v5, /device:TPU:1, one launch (start us, length us, event | category | flops | bytes accessed | tf_op | source)
XLA Modules:
  0.0 84.8 jit_solution(9311150248667458855)
XLA Ops:
  0.6 82.9 %shard_map.58 = (f32[448,256]{1,0:T(8,128)S(1)}, f32[448,128]{1,0:T(8,128)S(1)}, f32[128,256]{1,0:T(8,128)S(1)}, f32[1,128]{1,0:T(1,128)S(1)}) custom-call(f32[448,256]{1,0:T(8,128)} %bitcast.8, bf16[448,256]{1,0:T(8,128)(2,1)} %bitcast.9, f32[448,128]{1,0:T(8,128)} %bitcast.10), custom_call_target="tpu_custom_call" | custom-call | tf_op jit(solution)/shard_map/pallas_call | solution.py:292
  83.5 1.2 %shard_map.59 = (f32[448,256]{1,0:T(8,128)}, f32[448,128]{1,0:T(8,128)}, f32[448,256]{1,0:T(8,128)}) custom-call(f32[448,256]{1,0:T(8,128)S(1)} %get-tuple-element.10.moment, f32[448,128]{1,0:T(8,128)S(1)} %get-tuple-element.11.right_tall, f32[128,256]{1,0:T(8,128)S(1)} %get-tuple-element.12.left, f32[1,128]{1,0:T(1,128)S(1)} %get-tuple-element.13.norm), custom_call_target="tpu_custom_call" | custom-call | tf_op jit(solution)/shard_map/pallas_call | solution.py:339

commit v6 on v5

--- a/solution.py
+++ b/solution.py
@@ -276,9 +276,17 @@
     stores.append(pltpu.make_async_copy(factor_v, new_factor, out_sem.at[1]))
     stores[-1].start()
     span = WIDE // 4
+    scaled = left[...] * SCALE
+    left_high = scaled.astype(jnp.bfloat16)
+    left_low = (scaled - left_high.astype(jnp.float32)).astype(jnp.bfloat16)
+    stacked = jnp.concatenate([left_high, left_high], axis=0)
     for k in range(4):
         rows = pl.ds(k * span, span)
-        update_v[rows, :] = contract(factor_v[rows, :] * SCALE, left[...], 1, 0)
+        part = factor_v[rows, :]
+        high = part.astype(jnp.bfloat16)
+        low = (part - high.astype(jnp.float32)).astype(jnp.bfloat16)
+        main = jnp.dot(jnp.concatenate([high, low], axis=1), stacked, preferred_element_type=jnp.float32)
+        update_v[rows, :] = main + jnp.dot(high, left_low, preferred_element_type=jnp.float32)
         stores.append(pltpu.make_async_copy(update_v.at[rows], update.at[rows], out_sem.at[k + 2]))
         stores[-1].start()
     for store in stores:

time: 84.9 us -> 84.7 us (level)
  no operation moved by 1% of the time
where the time goes in v6:
time: 84.7 us; the launch traced here: 84.6 us
  Pallas kernels  83.9 us (99%)
    pallas_call x1, Pallas kernels, local(): pl.pallas_call(kernel, out_shape=(jax.ShapeDtypeStruct((WIDE, HIGH), f32)...  82.9 us

profile of v6, /device:TPU:1, one launch (start us, length us, event | category | flops | bytes accessed | tf_op | source)
XLA Modules:
  0.0 84.6 jit_solution(1070489107304284961)
XLA Ops:
  0.6 82.9 %shard_map.58 = (f32[448,256]{1,0:T(8,128)S(1)}, f32[448,128]{1,0:T(8,128)S(1)}, f32[128,256]{1,0:T(8,128)S(1)}, f32[1,128]{1,0:T(1,128)S(1)}) custom-call(f32[448,256]{1,0:T(8,128)} %bitcast.8, bf16[448,256]{1,0:T(8,128)(2,1)} %bitcast.9, f32[448,128]{1,0:T(8,128)} %bitcast.10), custom_call_target="tpu_custom_call" | custom-call | tf_op jit(solution)/shard_map/pallas_call | solution.py:300
  83.5 1.0 %shard_map.59 = (f32[448,256]{1,0:T(8,128)}, f32[448,128]{1,0:T(8,128)}, f32[448,256]{1,0:T(8,128)}) custom-call(f32[448,256]{1,0:T(8,128)S(1)} %get-tuple-element.10.moment, f32[448,128]{1,0:T(8,128)S(1)} %get-tuple-element.11.right_tall, f32[128,256]{1,0:T(8,128)S(1)} %get-tuple-element.12.left, f32[1,128]{1,0:T(1,128)S(1)} %get-tuple-element.13.norm), custom_call_target="tpu_custom_call" | custom-call | tf_op jit(solution)/shard_map/pallas_call | solution.py:347

commit v7 on v6

--- a/solution.py
+++ b/solution.py
@@ -248,11 +248,13 @@
 
     lax.fori_loop(0, POWER, sweep, 0)
 
-    right_tall[...] = right[...].T
-    square_own[...] = jnp.sum(right_tall[...] * right_tall[...], axis=0, keepdims=True)
+    spot = lax.broadcasted_iota(jnp.int32, (RANK, RANK), 0) == lax.broadcasted_iota(jnp.int32, (RANK, RANK), 1)
+    squares = jnp.sum(right[...] * right[...], axis=1, keepdims=True)
+    square_own[...] = jnp.sum(jnp.where(spot, jnp.broadcast_to(squares, (RANK, RANK)), 0.0), axis=0, keepdims=True)
     square_got[col] = square_own[...]
     for peer in col_peers:
         remote(square_own, square_got.at[col], square_send, square_recv, (row, peer))
+    right_tall[...] = right[...].T
     left[:, :HALF] = contract(gram[last], left_h[last, 0], 1, 0)
     left[:, HALF:] = contract(gram[last], left_h[last, 1], 1, 0)
     moment[...] = tall[...] - DECAY_LEFT * contract(right_tall[...], left[...], 1, 0)

time: 84.7 us -> 84.5 us (level)
  no operation moved by 1% of the time
where the time goes in v7:
time: 84.5 us; the launch traced here: 84.4 us
  Pallas kernels  83.7 us (99%)
    pallas_call x1, Pallas kernels, local(): pl.pallas_call(kernel, out_shape=(jax.ShapeDtypeStruct((WIDE, HIGH), f32)...  82.7 us

profile of v7, /device:TPU:1, one launch (start us, length us, event | category | flops | bytes accessed | tf_op | source)
XLA Modules:
  0.0 84.4 jit_solution(16088683607515892230)
XLA Ops:
  0.6 82.7 %shard_map.58 = (f32[448,256]{1,0:T(8,128)S(1)}, f32[448,128]{1,0:T(8,128)S(1)}, f32[128,256]{1,0:T(8,128)S(1)}, f32[1,128]{1,0:T(1,128)S(1)}) custom-call(f32[448,256]{1,0:T(8,128)} %bitcast.8, bf16[448,256]{1,0:T(8,128)(2,1)} %bitcast.9, f32[448,128]{1,0:T(8,128)} %bitcast.10), custom_call_target="tpu_custom_call" | custom-call | tf_op jit(solution)/shard_map/pallas_call | solution.py:302
  83.3 1.0 %shard_map.59 = (f32[448,256]{1,0:T(8,128)}, f32[448,128]{1,0:T(8,128)}, f32[448,256]{1,0:T(8,128)}) custom-call(f32[448,256]{1,0:T(8,128)S(1)} %get-tuple-element.10.moment, f32[448,128]{1,0:T(8,128)S(1)} %get-tuple-element.11.right_tall, f32[128,256]{1,0:T(8,128)S(1)} %get-tuple-element.12.left, f32[1,128]{1,0:T(1,128)S(1)} %get-tuple-element.13.norm), custom_call_target="tpu_custom_call" | custom-call | tf_op jit(solution)/shard_map/pallas_call | solution.py:349
